TPU v7x, 32 devices: a whole 2x2x4 slice. The times are simulated.
32 devices in a mesh: head: 4 (over z), outer: 2 (over core), inner: 4 (over y, x).
Axes of the slice: x: 2, y: 2, z: 4, core: 2. Of those that a mesh axis runs over, the one named last changes fastest.
Arguments:
- query_in: bfloat16 [8, 384, 1024], P(('outer', 'inner'), 'head'), may hold values from -48 to 48
- key_in: bfloat16 [8, 384, 512], P(('outer', 'inner'), 'head'), may hold values from -6 to 6
- value_in: bfloat16 [8, 384, 512], P(('outer', 'inner'), 'head'), may hold values from -6 to 6
- grad_out: bfloat16 [8, 384, 1024], P(('outer', 'inner'), 'head'), may hold values from -48 to 48
Outputs:
- grad_query: bfloat16 [8, 384, 1024], P(('outer', 'inner'), 'head')
- grad_key: bfloat16 [8, 384, 512], P(('outer', 'inner'), 'head')
- grad_value: bfloat16 [8, 384, 512], P(('outer', 'inner'), 'head')
All inputs are finite; a program needn't handle non-finite values.
Results may differ from a plain program's by a relative error of at most 0.0058.
Values may be sent and summed in bfloat16 or wider, within the bound.
A program may use at most 128 MiB of HBM per device.

v0:
```python
import jax
import jax.numpy as jnp
from jax import lax
from jax.sharding import PartitionSpec as P

HD = 128
GROUP = 2
WINDOW = 4096


SOFT_CAP = 50.0
QUERY_SCALE = 1.0 / 12.0


def passed_along(shard, axis, by):
    length = lax.axis_size(axis)
    pairs = [(i, i + by) for i in range(length) if 0 <= i + by < length]
    return lax.ppermute(shard, axis, pairs)


def slot_mask(position, slot_index, tok_rows):
    query_pos = position * tok_rows + lax.broadcasted_iota(jnp.int32, (tok_rows, tok_rows), 0)
    key_pos = (position - slot_index) * tok_rows + lax.broadcasted_iota(
        jnp.int32, (tok_rows, tok_rows), 1
    )
    return (key_pos <= query_pos) & (key_pos > query_pos - WINDOW) & (key_pos >= 0)


def first_terms(running, slot_index, kv_block, queries, out_grads, position):
    tanh_all, prob_grads, totals, weighted = running
    tok_rows = queries.shape[0]
    kv_count = queries.shape[1]
    split_kv = kv_block.reshape(tok_rows, kv_count, 2, HD)
    scores = jnp.einsum(
        "tagd,kad->agtk", queries, split_kv[:, :, 0], preferred_element_type=jnp.float32
    )
    capped = jnp.tanh(scores * (QUERY_SCALE / SOFT_CAP))
    grad_prob = jnp.einsum(
        "tagd,kad->agtk", out_grads, split_kv[:, :, 1], preferred_element_type=jnp.float32
    ).astype(jnp.bfloat16)
    allowed = slot_mask(position, slot_index, tok_rows)
    weights = jnp.where(allowed, jnp.exp(SOFT_CAP * capped), 0.0)
    totals = totals + jnp.sum(weights, axis=3)
    weighted = weighted + jnp.sum(weights * grad_prob.astype(jnp.float32), axis=3)
    tanh_all = lax.dynamic_update_index_in_dim(tanh_all, capped, slot_index, 0)
    prob_grads = lax.dynamic_update_index_in_dim(prob_grads, grad_prob, slot_index, 0)
    return (tanh_all, prob_grads, totals, weighted)


def second_terms(
    slot_index, kv_block, tanh_all, prob_grads, totals, row_delta, queries, out_grads, position
):
    tok_rows = queries.shape[0]
    kv_count = queries.shape[1]
    split_kv = kv_block.reshape(tok_rows, kv_count, 2, HD)
    capped = lax.dynamic_index_in_dim(tanh_all, slot_index, 0, keepdims=False)
    grad_prob = lax.dynamic_index_in_dim(prob_grads, slot_index, 0, keepdims=False).astype(
        jnp.float32
    )
    allowed = slot_mask(position, slot_index, tok_rows)
    weights = jnp.where(allowed, jnp.exp(SOFT_CAP * capped), 0.0)
    attn_prob = weights / totals[..., None]
    grad_value = jnp.einsum(
        "agtk,tagd->kad",
        attn_prob.astype(jnp.bfloat16),
        out_grads,
        preferred_element_type=jnp.float32,
    )
    scaled = (
        attn_prob * (grad_prob - row_delta[..., None]) * (QUERY_SCALE * (1.0 - capped * capped))
    ).astype(jnp.bfloat16)
    query_term = jnp.einsum(
        "agtk,kad->tagd", scaled, split_kv[:, :, 0], preferred_element_type=jnp.float32
    )
    grad_key = jnp.einsum("agtk,tagd->kad", scaled, queries, preferred_element_type=jnp.float32)
    kv_term = jnp.stack([grad_key, grad_value], axis=2).reshape(tok_rows, kv_count * 2 * HD)
    return (query_term, kv_term)


def body(query_in, key_in, value_in, grad_out):
    query_in, grad_out, key_in, value_in = (
        lax.all_to_all(query_in, "head", split_axis=2, concat_axis=1, tiled=True),
        lax.all_to_all(grad_out, "head", split_axis=2, concat_axis=1, tiled=True),
        lax.all_to_all(key_in, "head", split_axis=2, concat_axis=1, tiled=True),
        lax.all_to_all(value_in, "head", split_axis=2, concat_axis=1, tiled=True),
    )
    tok_rows = query_in.shape[1]
    kv_count = key_in.shape[2] // HD
    queries = query_in[0].reshape(tok_rows, kv_count, GROUP, HD)
    out_grads = grad_out[0].reshape(tok_rows, kv_count, GROUP, HD)
    key_value = jnp.stack(
        [key_in[0].reshape(tok_rows, kv_count, HD), value_in[0].reshape(tok_rows, kv_count, HD)],
        axis=2,
    ).reshape(tok_rows, kv_count * 2 * HD)
    kv_width = key_value.shape[1]
    lookback = (WINDOW + tok_rows - 2) // tok_rows
    slot_count = lookback + 1
    position = lax.axis_index(("outer", "inner"))
    running = (
        jnp.zeros((slot_count, kv_count, GROUP, tok_rows, tok_rows), jnp.float32),
        jnp.zeros((slot_count, kv_count, GROUP, tok_rows, tok_rows), jnp.bfloat16),
        jnp.zeros((kv_count, GROUP, tok_rows), jnp.float32),
        jnp.zeros((kv_count, GROUP, tok_rows), jnp.float32),
    )
    dquery = jnp.zeros((tok_rows, kv_count, GROUP, HD), jnp.float32)
    sections = []
    filled = 1
    while filled < slot_count:
        extra = min(filled, slot_count - filled)
        sections.append((filled, extra))
        filled = filled + extra
    window = key_value[None]
    for filled, extra in sections:
        arrived = passed_along(window[:extra], ("outer", "inner"), filled)
        window = jnp.concatenate([window, arrived], axis=0)

    def forward_local(slot_index, inner_stats):
        kv_slot = lax.dynamic_index_in_dim(window, slot_index, 0, keepdims=False)
        return first_terms(inner_stats, slot_index, kv_slot, queries, out_grads, position)

    running = lax.fori_loop(0, slot_count, forward_local, running)
    tanh_all, prob_grads, totals, weighted = running
    row_delta = weighted / totals

    def backward_local(slot_index, loop_carry):
        collected, query_acc = loop_carry
        kv_slot = lax.dynamic_index_in_dim(window, slot_index, 0, keepdims=False)
        query_term, kv_term = second_terms(
            slot_index,
            kv_slot,
            tanh_all,
            prob_grads,
            totals,
            row_delta,
            queries,
            out_grads,
            position,
        )
        collected = lax.dynamic_update_index_in_dim(collected, kv_term, slot_index, 0)
        return (collected, query_acc + query_term)

    collected, dquery = lax.fori_loop(
        0,
        slot_count,
        backward_local,
        (jnp.zeros((slot_count, tok_rows, kv_width), jnp.float32), dquery),
    )
    for filled, extra in reversed(sections):
        returned = passed_along(collected[filled : filled + extra], ("outer", "inner"), -filled)
        collected = jnp.concatenate([collected[:extra] + returned, collected[extra:filled]], axis=0)
    own_grads = collected[0]
    split_grads = own_grads.reshape(tok_rows, kv_count, 2, HD)
    grad_query = dquery.reshape(1, tok_rows, kv_count * GROUP * HD).astype(jnp.bfloat16)
    grad_key = split_grads[:, :, 0].reshape(1, tok_rows, kv_count * HD).astype(jnp.bfloat16)
    grad_value = split_grads[:, :, 1].reshape(1, tok_rows, kv_count * HD).astype(jnp.bfloat16)
    grad_query, grad_key, grad_value = (
        lax.all_to_all(grad_query, "head", split_axis=1, concat_axis=2, tiled=True),
        lax.all_to_all(grad_key, "head", split_axis=1, concat_axis=2, tiled=True),
        lax.all_to_all(grad_value, "head", split_axis=1, concat_axis=2, tiled=True),
    )
    return (grad_query, grad_key, grad_value)


def solution(mesh):
    in_specs = (
        P(("outer", "inner"), "head", None),
        P(("outer", "inner"), "head", None),
        P(("outer", "inner"), "head", None),
        P(("outer", "inner"), "head", None),
    )
    out_specs = (
        P(("outer", "inner"), "head", None),
        P(("outer", "inner"), "head", None),
        P(("outer", "inner"), "head", None),
    )
    return jax.shard_map(body, mesh=mesh, in_specs=in_specs, out_specs=out_specs, check_vma=False)
```

profile of v0, /device:TPU:0, one launch (start us, length us, event | category | flops | bytes accessed | tf_op | source)
XLA Modules:
  0.0 275.4 jit_solution(5899292727773802666)
XLA Ops:
  4.6 6.3 %all-to-all-start = ((bf16[4,2,6144]{2,1,0:T(2,128)(2,1)}), bf16[4,2,6144]{2,1,0:T(2,128)(2,1)S(1)}, u32[]{:S(2)}, u32[]{:S(2)}) async-start(bf16[4,2,6144]{2,1,0:T(2,128)(2,1)} %reshape.278), calls=%async_computation | async-start | bytes 196608 | tf_op jit(solution)/shard_map/all_to_all | solution.py:84
  13.4 3.4 %all-to-all-done = bf16[4,2,6144]{2,1,0:T(2,128)(2,1)S(1)} async-done(((bf16[4,2,6144]{2,1,0:T(2,128)(2,1)}), bf16[4,2,6144]{2,1,0:T(2,128)(2,1)S(1)}, u32[]{:S(2)}, u32[]{:S(2)}) %all-to-all-start) | async-done | bytes 98336 | tf_op jit(solution)/shard_map/all_to_all | solution.py:84
  16.8 3.3 %all-to-all-start.1 = ((bf16[4,2,6144]{2,1,0:T(2,128)(2,1)}), bf16[4,2,6144]{2,1,0:T(2,128)(2,1)S(1)}, u32[]{:S(2)}, u32[]{:S(2)}) async-start(bf16[4,2,6144]{2,1,0:T(2,128)(2,1)} %reshape.276), calls=%async_computation.1 | async-start | bytes 196608 | tf_op jit(solution)/shard_map/all_to_all | solution.py:85
  20.4 5.4 %all-to-all-done.1 = bf16[4,2,6144]{2,1,0:T(2,128)(2,1)S(1)} async-done(((bf16[4,2,6144]{2,1,0:T(2,128)(2,1)}), bf16[4,2,6144]{2,1,0:T(2,128)(2,1)S(1)}, u32[]{:S(2)}, u32[]{:S(2)}) %all-to-all-start.1) | async-done | bytes 98336 | tf_op jit(solution)/shard_map/all_to_all | solution.py:85
  26.5 3.4 %collective-permute-start = (bf16[1,384,256]{1,2,0:T(8,128)(2,1)S(1)}, bf16[1,384,256]{1,2,0:T(8,128)(2,1)S(1)}, u32[]{:S(2)}, u32[]{:S(2)}) collective-permute-start(bf16[1,384,256]{1,2,0:T(8,128)(2,1)S(1)} %bitcast.223), channel_id=1, source_target_pairs={{0,1},{1,2},{2,3},{3,4},{4,5},{5,6},{6,7},{8,9},{9,10},{10,11},{11... | collective-permute-start | bytes 589832 | tf_op jit(solution)/shard_map/ppermute | solution.py:18
  29.9 3.2 %collective-permute-done = bf16[1,384,256]{1,2,0:T(8,128)(2,1)S(1)} collective-permute-done((bf16[1,384,256]{1,2,0:T(8,128)(2,1)S(1)}, bf16[1,384,256]{1,2,0:T(8,128)(2,1)S(1)}, u32[]{:S(2)}, u32[]{:S(2)}) %collective-permute-start) | collective-permute-done | bytes 196640 | tf_op jit(solution)/shard_map/ppermute | solution.py:18
  33.1 5.3 %collective-permute-start.1 = (bf16[2,384,256]{1,2,0:T(8,128)(2,1)S(1)}, bf16[2,384,256]{1,2,0:T(8,128)(2,1)S(1)}, u32[]{:S(2)}, u32[]{:S(2)}) collective-permute-start(bf16[2,384,256]{1,2,0:T(8,128)(2,1)S(1)} %pad_maximum_fusion.2), channel_id=1, source_target_pairs={{0,2},{1,3},{2,4},{3,5},{4,6},{5,7},{8,10},{9,11},{10,12},{11,13},... | collective-permute-start | bytes 1179656 | tf_op jit(solution)/shard_map/ppermute | solution.py:18
  38.8 2.2 reduce.14
  42.2 3.4 %all-to-all-start.2 = ((bf16[4,2,12288]{2,1,0:T(2,128)(2,1)}), bf16[4,2,12288]{2,1,0:T(2,128)(2,1)S(1)}, u32[]{:S(2)}, u32[]{:S(2)}) async-start(bf16[4,2,12288]{2,1,0:T(2,128)(2,1)} %reshape.280), calls=%async_computation.2 | async-start | bytes 393216 | tf_op jit(solution)/shard_map/all_to_all | solution.py:82
  45.7 2.2 collective-permute-start.2
  49.0 2.2 reduce.15
  52.4 5.0 %all-to-all-start.3 = ((bf16[4,2,12288]{2,1,0:T(2,128)(2,1)}), bf16[4,2,12288]{2,1,0:T(2,128)(2,1)S(1)}, u32[]{:S(2)}, u32[]{:S(2)}) async-start(bf16[4,2,12288]{2,1,0:T(2,128)(2,1)} %reshape.282), calls=%async_computation.3 | async-start | bytes 393216 | tf_op jit(solution)/shard_map/all_to_all | solution.py:83
  59.4 4.3 %all-to-all-done.3 = bf16[4,2,12288]{2,1,0:T(2,128)(2,1)S(1)} async-done(((bf16[4,2,12288]{2,1,0:T(2,128)(2,1)}), bf16[4,2,12288]{2,1,0:T(2,128)(2,1)S(1)}, u32[]{:S(2)}, u32[]{:S(2)}) %all-to-all-start.3) | async-done | bytes 196640 | tf_op jit(solution)/shard_map/all_to_all | solution.py:83
  66.4 2.1 constant_dynamic-update-slice_fusion.2
  69.5 50.3 %while.40 = (s32[]{:T(128)}, f32[12,1,2,384,384]{3,4,2,1,0:T(8,128)}, bf16[12,1,2,384,384]{3,4,2,1,0:T(8,128)(2,1)}, f32[1,2,384]{2,1,0:T(2,128)S(1)}, f32[1,2,3...) while((s32[]{:T(128)}, ...), condition=%wide.region_3.4_spmd.clone, body=%wide.region_0.3_spmd.clone.sunk | while | flops 153947904 | bytes 6622131 | solution.py:121
  119.8 89.0 %while.41 = (s32[]{:T(128)}, f32[12,384,256]{1,2,0:T(8,128)}, f32[384,1,2,128]{0,3,2,1:T(8,128)S(1)}, s32[]{:T(128)}, s32[]{:T(128)}, /*index=5*/f32[12,1,2,384,...) while((s32[]{:T(128)}, f32[12,384,256]{1,2,0:T(8,128)}, ...), condition=%wide.region_5.6_spmd.clone, body=%wide.region_4.5_spmd.clone.sunk | while | flops 235046784 | bytes 16049607 | solution.py:142
  213.0 4.0 %collective-permute-done.5 = f32[4,384,256]{1,2,0:T(8,128)S(1)} collective-permute-done((f32[4,384,256]{1,2,0:T(8,128)S(1)}, f32[4,384,256]{1,2,0:T(8,128)S(1)}, u32[]{:S(2)}, u32[]{:S(2)}) %collective-permute-start.5) | collective-permute-done | bytes 1572896 | tf_op jit(solution)/shard_map/ppermute | solution.py:18
  220.1 20.2 %collective-permute-done.6 = f32[2,384,256]{1,2,0:T(8,128)S(1)} collective-permute-done((f32[2,384,256]{1,2,0:T(8,128)S(1)}, f32[2,384,256]{1,2,0:T(8,128)S(1)}, u32[]{:S(2)}, u32[]{:S(2)}) %collective-permute-start.6) | collective-permute-done | bytes 786464 | tf_op jit(solution)/shard_map/ppermute | solution.py:18
  244.8 3.4 %all-to-all-start.4 = ((bf16[4,2,12288]{2,1,0:T(2,128)(2,1)}), bf16[4,2,12288]{2,1,0:T(2,128)(2,1)S(1)}, u32[]{:S(2)}, u32[]{:S(2)}) async-start(bf16[4,2,12288]{2,1,0:T(2,128)(2,1)} %reshape.284), calls=%async_computation.4 | async-start | bytes 393216 | tf_op jit(solution)/shard_map/all_to_all | solution.py:157
  248.2 4.4 %collective-permute-done.7 = f32[1,384,256]{1,2,0:T(8,128)S(1)} collective-permute-done((f32[1,384,256]{1,2,0:T(8,128)S(1)}, f32[1,384,256]{1,2,0:T(8,128)S(1)}, u32[]{:S(2)}, u32[]{:S(2)}) %collective-permute-start.7) | collective-permute-done | bytes 393248 | tf_op jit(solution)/shard_map/ppermute | solution.py:18
  256.4 3.3 %all-to-all-start.5 = ((bf16[4,2,6144]{2,1,0:T(2,128)(2,1)}), bf16[4,2,6144]{2,1,0:T(2,128)(2,1)S(1)}, u32[]{:S(2)}, u32[]{:S(2)}) async-start(bf16[4,2,6144]{2,1,0:T(2,128)(2,1)} %reshape.286), calls=%async_computation.5 | async-start | bytes 196608 | tf_op jit(solution)/shard_map/all_to_all | solution.py:158
  261.8 3.8 %all-to-all-done.5 = bf16[4,2,6144]{2,1,0:T(2,128)(2,1)S(1)} async-done(((bf16[4,2,6144]{2,1,0:T(2,128)(2,1)}), bf16[4,2,6144]{2,1,0:T(2,128)(2,1)S(1)}, u32[]{:S(2)}, u32[]{:S(2)}) %all-to-all-start.5) | async-done | bytes 98336 | tf_op jit(solution)/shard_map/all_to_all | solution.py:158
  265.5 3.3 %all-to-all-start.6 = ((bf16[4,2,6144]{2,1,0:T(2,128)(2,1)}), bf16[4,2,6144]{2,1,0:T(2,128)(2,1)S(1)}, u32[]{:S(2)}, u32[]{:S(2)}) async-start(bf16[4,2,6144]{2,1,0:T(2,128)(2,1)} %reshape.288), calls=%async_computation.6 | async-start | bytes 196608 | tf_op jit(solution)/shard_map/all_to_all | solution.py:159
  269.9 4.8 %all-to-all-done.6 = bf16[4,2,6144]{2,1,0:T(2,128)(2,1)S(1)} async-done(((bf16[4,2,6144]{2,1,0:T(2,128)(2,1)}), bf16[4,2,6144]{2,1,0:T(2,128)(2,1)S(1)}, u32[]{:S(2)}, u32[]{:S(2)}) %all-to-all-start.6) | async-done | bytes 98336 | tf_op jit(solution)/shard_map/all_to_all | solution.py:159
  (380 shorter events, 173.3 us)
Async XLA Ops:
  0.6 10.3 %copy-start.3 = (bf16[1,96,512]{2,1,0:T(8,128)(2,1)S(1)}, bf16[1,96,512]{2,1,0:T(8,128)(2,1)}, u32[]{:S(2)}) copy-start(bf16[1,96,512]{2,1,0:T(8,128)(2,1)} %param.10) | copy-start | bytes 294916
  4.6 12.2 %all-to-all-start = ((bf16[4,2,6144]{2,1,0:T(2,128)(2,1)}), bf16[4,2,6144]{2,1,0:T(2,128)(2,1)S(1)}, u32[]{:S(2)}, u32[]{:S(2)}) async-start(bf16[4,2,6144]{2,1,0:T(2,128)(2,1)} %reshape.278), calls=%async_computation | async-start | bytes 196608 | tf_op jit(solution)/shard_map/all_to_all | solution.py:84
  16.8 9.1 %all-to-all-start.1 = ((bf16[4,2,6144]{2,1,0:T(2,128)(2,1)}), bf16[4,2,6144]{2,1,0:T(2,128)(2,1)S(1)}, u32[]{:S(2)}, u32[]{:S(2)}) async-start(bf16[4,2,6144]{2,1,0:T(2,128)(2,1)} %reshape.276), calls=%async_computation.1 | async-start | bytes 196608 | tf_op jit(solution)/shard_map/all_to_all | solution.py:85
  26.1 12.4 %copy-start.1 = (bf16[1,96,1024]{2,1,0:T(8,128)(2,1)S(1)}, bf16[1,96,1024]{2,1,0:T(8,128)(2,1)}, u32[]{:S(2)}) copy-start(bf16[1,96,1024]{2,1,0:T(8,128)(2,1)} %param.8) | copy-start | bytes 589828
  26.5 6.6 %collective-permute-start = (bf16[1,384,256]{1,2,0:T(8,128)(2,1)S(1)}, bf16[1,384,256]{1,2,0:T(8,128)(2,1)S(1)}, u32[]{:S(2)}, u32[]{:S(2)}) collective-permute-start(bf16[1,384,256]{1,2,0:T(8,128)(2,1)S(1)} %bitcast.223), channel_id=1, source_target_pairs={{0,1},{1,2},{2,3},{3,4},{4,5},{5,6},{6,7},{8,9},{9,10},{10,11},{11... | collective-permute-start | bytes 589832 | tf_op jit(solution)/shard_map/ppermute | solution.py:18
  33.1 12.5 %collective-permute-start.1 = (bf16[2,384,256]{1,2,0:T(8,128)(2,1)S(1)}, bf16[2,384,256]{1,2,0:T(8,128)(2,1)S(1)}, u32[]{:S(2)}, u32[]{:S(2)}) collective-permute-start(bf16[2,384,256]{1,2,0:T(8,128)(2,1)S(1)} %pad_maximum_fusion.2), channel_id=1, source_target_pairs={{0,2},{1,3},{2,4},{3,5},{4,6},{5,7},{8,10},{9,11},{10,12},{11,13},... | collective-permute-start | bytes 1179656 | tf_op jit(solution)/shard_map/ppermute | solution.py:18
  41.1 7.5 %copy-start.2 = (bf16[1,96,1024]{2,1,0:T(8,128)(2,1)S(1)}, bf16[1,96,1024]{2,1,0:T(8,128)(2,1)}, u32[]{:S(2)}) copy-start(bf16[1,96,1024]{2,1,0:T(8,128)(2,1)} %param.11) | copy-start | bytes 589828
  42.2 10.2 %all-to-all-start.2 = ((bf16[4,2,12288]{2,1,0:T(2,128)(2,1)}), bf16[4,2,12288]{2,1,0:T(2,128)(2,1)S(1)}, u32[]{:S(2)}, u32[]{:S(2)}) async-start(bf16[4,2,12288]{2,1,0:T(2,128)(2,1)} %reshape.280), calls=%async_computation.2 | async-start | bytes 393216 | tf_op jit(solution)/shard_map/all_to_all | solution.py:82
  45.7 20.7 %collective-permute-start.2 = (bf16[4,384,256]{1,2,0:T(8,128)(2,1)S(1)}, bf16[4,384,256]{1,2,0:T(8,128)(2,1)}, u32[]{:S(2)}, u32[]{:S(2)}) collective-permute-start(bf16[4,384,256]{1,2,0:T(8,128)(2,1)S(1)} %pad_maximum_fusion.1), channel_id=1, source_target_pairs={{0,4},{1,5},{2,6},{3,7},{8,12},{9,13},{10,14},{11,15},{16,20},{17,... | collective-permute-start | bytes 2359304 | tf_op jit(solution)/shard_map/ppermute | solution.py:18
  47.9 20.6 %collective-permute-start.3 = (bf16[4,384,256]{1,2,0:T(8,128)(2,1)S(1)}, bf16[4,384,256]{1,2,0:T(8,128)(2,1)S(1)}, u32[]{:S(2)}, u32[]{:S(2)}) collective-permute-start(bf16[4,384,256]{1,2,0:T(8,128)(2,1)S(1)} %pad_maximum_fusion.1), channel_id=1, source_target_pairs={} | collective-permute-start | bytes 2359304 | tf_op jit(solution)/shard_map/ppermute | solution.py:18
  52.4 11.3 %all-to-all-start.3 = ((bf16[4,2,12288]{2,1,0:T(2,128)(2,1)}), bf16[4,2,12288]{2,1,0:T(2,128)(2,1)S(1)}, u32[]{:S(2)}, u32[]{:S(2)}) async-start(bf16[4,2,12288]{2,1,0:T(2,128)(2,1)} %reshape.282), calls=%async_computation.3 | async-start | bytes 393216 | tf_op jit(solution)/shard_map/all_to_all | solution.py:83
  69.5 50.3 %copy-start = (f32[384,1,2,128]{0,3,2,1:T(8,128)S(1)}, f32[384,1,2,128]{0,3,2,1:T(8,128)}, u32[]{:S(2)}) copy-start(f32[384,1,2,128]{0,3,2,1:T(8,128)} %custom-call.2) | copy-start | bytes 1179652
  210.9 2.1 collective-permute-start.4
  211.7 5.3 %collective-permute-start.5 = (f32[4,384,256]{1,2,0:T(8,128)S(1)}, f32[4,384,256]{1,2,0:T(8,128)S(1)}, u32[]{:S(2)}, u32[]{:S(2)}) collective-permute-start(f32[4,384,256]{1,2,0:T(8,128)S(1)} %get-tuple-element.746), channel_id=1, source_target_pairs={{4,0},{5,1},{6,2},{7,3},{12,8},{13,9},{14,10},{15,11},{20,16},{21,... | collective-permute-start | bytes 4718600 | tf_op jit(solution)/shard_map/ppermute | solution.py:18
  218.8 21.5 %collective-permute-start.6 = (f32[2,384,256]{1,2,0:T(8,128)S(1)}, f32[2,384,256]{1,2,0:T(8,128)S(1)}, u32[]{:S(2)}, u32[]{:S(2)}) collective-permute-start(f32[2,384,256]{1,2,0:T(8,128)S(1)} %slice.75), channel_id=1, source_target_pairs={{2,0},{3,1},{4,2},{5,3},{6,4},{7,5},{10,8},{11,9},{12,10},{13,11},... | collective-permute-start | bytes 2359304 | tf_op jit(solution)/shard_map/ppermute | solution.py:18
  240.4 12.2 %collective-permute-start.7 = (f32[1,384,256]{1,2,0:T(8,128)S(1)}, f32[1,384,256]{1,2,0:T(8,128)S(1)}, u32[]{:S(2)}, u32[]{:S(2)}) collective-permute-start(f32[1,384,256]{1,2,0:T(8,128)S(1)} %slice.77), channel_id=1, source_target_pairs={{1,0},{2,1},{3,2},{4,3},{5,4},{6,5},{7,6},{9,8},{10,9},{11,10},{12... | collective-permute-start | bytes 1179656 | tf_op jit(solution)/shard_map/ppermute | solution.py:18
  244.8 11.6 %all-to-all-start.4 = ((bf16[4,2,12288]{2,1,0:T(2,128)(2,1)}), bf16[4,2,12288]{2,1,0:T(2,128)(2,1)S(1)}, u32[]{:S(2)}, u32[]{:S(2)}) async-start(bf16[4,2,12288]{2,1,0:T(2,128)(2,1)} %reshape.284), calls=%async_computation.4 | async-start | bytes 393216 | tf_op jit(solution)/shard_map/all_to_all | solution.py:157
  256.4 9.1 %all-to-all-start.5 = ((bf16[4,2,6144]{2,1,0:T(2,128)(2,1)}), bf16[4,2,6144]{2,1,0:T(2,128)(2,1)S(1)}, u32[]{:S(2)}, u32[]{:S(2)}) async-start(bf16[4,2,6144]{2,1,0:T(2,128)(2,1)} %reshape.286), calls=%async_computation.5 | async-start | bytes 196608 | tf_op jit(solution)/shard_map/all_to_all | solution.py:158
  265.5 9.1 %all-to-all-start.6 = ((bf16[4,2,6144]{2,1,0:T(2,128)(2,1)}), bf16[4,2,6144]{2,1,0:T(2,128)(2,1)S(1)}, u32[]{:S(2)}, u32[]{:S(2)}) async-start(bf16[4,2,6144]{2,1,0:T(2,128)(2,1)} %reshape.288), calls=%async_computation.6 | async-start | bytes 196608 | tf_op jit(solution)/shard_map/all_to_all | solution.py:159
where the time goes:
time: 278 us; the launch traced here: 275 us
  local copies, waits for them, and re-layouts  92.4 us (33%)
  matrix products  56.8 us (20%)
  waiting for transfers between devices  55.1 us (20%)
  starting transfers between devices  44.3 us (16%)
  other arithmetic  23.7 us (9%)
    ppermute x8, waiting for transfers between devices, passed_along(): return lax.ppermute(shard, axis, pairs)  31.8 us
    dynamic_slice x24, local copies, waits for them, and re-layouts, second_terms(): capped = lax.dynamic_index_in_dim(tanh_all, slot_index, 0, keepdims=False)  20.6 us
    dynamic_slice x24, local copies, waits for them, and re-layouts, second_terms(): lax.dynamic_index_in_dim(prob_grads, slot_index, 0, keepdims=False)  17.3 us
    dot_general x12, matrix products, first_terms(): jnp.einsum('tagd,kad->agtk', queries, split_kv[:, :, 0], preferred_elemen...  16.8 us
    ppermute x8, starting transfers between devices, passed_along(): return lax.ppermute(shard, axis, pairs)  16.2 us
    unnamed x38, local copies, waits for them, and re-layouts  15 us
    dot_general x12, matrix products, first_terms(): jnp.einsum('tagd,kad->agtk', out_grads, split_kv[:, :, 1], preferred_elem...  14 us
    unnamed x10, other arithmetic  11.5 us
  transfers between devices with their start and end apart: 15, of which 10 were waited for; matrix products, arithmetic and copies ran while one was open for 9% of the time, Pallas kernels for 0%

commit v1 on v0

v1 whole, which is shorter than its diff:
```python
import functools

import jax
import jax.numpy as jnp
from jax import lax
from jax.experimental import pallas as pl
from jax.experimental.pallas import tpu as pltpu
from jax.sharding import PartitionSpec as P

HD = 128
GROUP = 2
WINDOW = 4096
SOFT_CAP = 50.0
QUERY_SCALE = 1.0 / 12.0
MESH = pl.DeviceIdType.MESH
KT = 128


def dot(a, b, ca, cb):
    return lax.dot_general(a, b, (((ca,), (cb,)), ((), ())), preferred_element_type=jnp.float32)


def kernel(
    heads, outer_n, inner_n, back,
    q_in, k_in, v_in, g_in,
    q_out, k_out, v_out,
    qs, gs, qst, gst, kv, e_all, c_all, d_all, tot, wgt, pb, sc, dqt, dq, dkv, dsend, drecv, own,
    a_send, a_recv, a_loc, b_send, b_recv, d_ssem, d_rsem, e_send, e_recv, e_loc,
):
    rows = q_in.shape[0]
    tok = rows * heads
    ctx = outer_n * inner_n
    h = lax.axis_index("head")
    pos = lax.axis_index("outer") * inner_n + lax.axis_index("inner")

    def at(t):
        return {"outer": lax.div(t, inner_n), "inner": lax.rem(t, inner_n)}

    def head_at(d):
        return lax.rem(h + d, heads)

    def part(who):
        return pl.ds(pl.multiple_of(who * rows, rows), rows)

    def lanes(who, width):
        return pl.ds(pl.multiple_of(who * width, width), width)

    barrier = pltpu.get_barrier_semaphore()
    for d in range(1, heads):
        pl.semaphore_signal(barrier, inc=1, device_id={"head": head_at(d)}, device_id_type=MESH)
    for s in range(1, back + 1):
        @pl.when(pos + s < ctx)
        def _():
            pl.semaphore_signal(barrier, inc=1, device_id=at(pos + s), device_id_type=MESH)

        @pl.when(pos - s >= 0)
        def _():
            pl.semaphore_signal(barrier, inc=1, device_id=at(pos - s), device_id_type=MESH)
    peers = heads - 1 + jnp.minimum(pos, back) + jnp.minimum(ctx - 1 - pos, back)
    pl.semaphore_wait(barrier, peers)

    srcs = ((k_in, HD), (v_in, HD), (q_in, GROUP * HD), (g_in, GROUP * HD))

    def dst_a(kind, who):
        if kind < 2:
            return kv.at[0, kind, part(who)]
        return (qs if kind == 2 else gs).at[part(who)]

    def copy_a(kind, d):
        ref, width = srcs[kind]
        return pltpu.make_async_remote_copy(
            src_ref=ref.at[:, lanes(head_at(d), width)],
            dst_ref=dst_a(kind, h),
            send_sem=a_send.at[kind, d], recv_sem=a_recv.at[kind, d],
            device_id={"head": head_at(d)}, device_id_type=MESH,
        )

    def arrival_a(kind, d):
        ref, width = srcs[kind]
        return pltpu.make_async_remote_copy(
            src_ref=ref.at[:, lanes(h, width)],
            dst_ref=dst_a(kind, head_at(heads - d)),
            send_sem=a_send.at[kind, d], recv_sem=a_recv.at[kind, d],
            device_id={"head": head_at(d)}, device_id_type=MESH,
        )

    def local_a(kind):
        ref, width = srcs[kind]
        return pltpu.make_async_copy(ref.at[:, lanes(h, width)], dst_a(kind, h), a_loc.at[kind])

    for kind in (0, 1):
        local_a(kind).start()
    for kind in (0, 1, 2, 3):
        for d in range(1, heads):
            copy_a(kind, d).start()
    for kind in (2, 3):
        local_a(kind).start()

    def copy_b(s, d):
        who = part(head_at(heads - d))
        return pltpu.make_async_remote_copy(
            src_ref=kv.at[0, :, who], dst_ref=kv.at[s, :, who],
            send_sem=b_send.at[s, d], recv_sem=b_recv.at[s, d],
            device_id=at(lax.rem(pos + s, ctx)), device_id_type=MESH,
        )

    for d in range(heads):
        for kind in (0, 1):
            if d == 0:
                local_a(kind).wait()
            else:
                arrival_a(kind, d).wait_recv()
        for s in range(1, back + 1):
            @pl.when(pos + s < ctx)
            def _():
                copy_b(s, d).start()

    for kind in (2, 3):
        local_a(kind).wait()
        for d in range(1, heads):
            arrival_a(kind, d).wait_recv()
    for j in range(GROUP):
        qst[j * tok:(j + 1) * tok] = qs[:, j * HD:(j + 1) * HD]
        gst[j * tok:(j + 1) * tok] = gs[:, j * HD:(j + 1) * HD]
    tot[...] = jnp.zeros_like(tot)
    wgt[...] = jnp.zeros_like(wgt)
    dqt[...] = jnp.zeros_like(dqt)

    free = (WINDOW - tok) // tok

    def first(s, masked):
        for t in range(tok // KT):
            at_t = slice(t * KT, (t + 1) * KT)
            keys = kv[s, 0, at_t]
            vals = kv[s, 1, at_t]
            for j in range(GROUP):
                col = slice(j * tok, (j + 1) * tok)
                capped = jnp.tanh(dot(keys, qst[col], 1, 1) * (QUERY_SCALE / SOFT_CAP))
                e = jnp.exp(SOFT_CAP * capped)
                if masked:
                    apart = (
                        s * tok - t * KT
                        + lax.broadcasted_iota(jnp.int32, e.shape, 1)
                        - lax.broadcasted_iota(jnp.int32, e.shape, 0)
                    )
                    e = jnp.where((apart >= 0) & (apart < WINDOW), e, 0.0)
                dp = dot(vals, gst[col], 1, 1).astype(jnp.bfloat16)
                c_all[s, at_t, col] = capped
                e_all[s, at_t, col] = e
                d_all[s, at_t, col] = dp
                tot[:, col] += jnp.sum(e.reshape(KT // 8, 8, tok), axis=0)
                wgt[:, col] += jnp.sum((e * dp.astype(jnp.float32)).reshape(KT // 8, 8, tok), axis=0)

    first(0, True)
    reach = jnp.minimum(pos, back)

    def first_step(masked, s, carry):
        for d in range(heads):
            copy_b(s, d).wait_recv()
        first(s, masked)
        return carry

    edge = jnp.minimum(reach, free)
    lax.fori_loop(1, edge + 1, functools.partial(first_step, False), 0)
    if back > free:
        lax.fori_loop(edge + 1, reach + 1, functools.partial(first_step, True), 0)

    total = jnp.sum(tot[...], axis=0, keepdims=True)
    inv = 1.0 / total
    delta = jnp.sum(wgt[...], axis=0, keepdims=True) * inv
    tot[0:1] = inv
    wgt[0:1] = delta

    def second(s):
        for t in range(tok // KT):
            at_t = slice(t * KT, (t + 1) * KT)
            for j in range(GROUP):
                col = slice(j * tok, (j + 1) * tok)
                capped = c_all[s, at_t, col]
                prob = e_all[s, at_t, col] * tot[0:1, col]
                pb[at_t, col] = prob.astype(jnp.bfloat16)
                diff = d_all[s, at_t, col].astype(jnp.float32) - wgt[0:1, col]
                sc[at_t, col] = (
                    prob * diff * (QUERY_SCALE - QUERY_SCALE * (capped * capped))
                ).astype(jnp.bfloat16)
        scaled = sc[...]
        dqt[...] += dot(kv[s, 0], scaled, 0, 0)
        return dot(scaled, qst[...], 1, 0), dot(pb[...], gst[...], 1, 0)

    def copy_d(s):
        return pltpu.make_async_remote_copy(
            src_ref=dsend.at[s - 1], dst_ref=drecv.at[s - 1],
            send_sem=d_ssem.at[s - 1], recv_sem=d_rsem.at[s - 1],
            device_id=at(lax.rem(pos - s + ctx, ctx)), device_id_type=MESH,
        )

    def second_step(i, carry):
        s = reach - i
        dk, dv = second(s)
        dsend[s - 1, 0] = dk.astype(jnp.bfloat16)
        dsend[s - 1, 1] = dv.astype(jnp.bfloat16)
        copy_d(s).start()
        return carry

    lax.fori_loop(0, reach, second_step, 0)
    dk, dv = second(0)
    own[0] = dk
    own[1] = dv
    for j in range(GROUP):
        dq[:, j * HD:(j + 1) * HD] = dqt[:, j * tok:(j + 1) * tok].T.astype(jnp.bfloat16)

    outs = ((q_out, GROUP * HD), (k_out, HD), (v_out, HD))

    def src_e(kind, who):
        return dq.at[part(who)] if kind == 0 else dkv.at[kind - 1, part(who)]

    def copy_e(kind, d):
        ref, width = outs[kind]
        return pltpu.make_async_remote_copy(
            src_ref=src_e(kind, head_at(d)), dst_ref=ref.at[:, lanes(h, width)],
            send_sem=e_send.at[kind, d], recv_sem=e_recv.at[kind, d],
            device_id={"head": head_at(d)}, device_id_type=MESH,
        )

    def arrival_e(kind, d):
        ref, width = outs[kind]
        return pltpu.make_async_remote_copy(
            src_ref=src_e(kind, h), dst_ref=ref.at[:, lanes(head_at(heads - d), width)],
            send_sem=e_send.at[kind, d], recv_sem=e_recv.at[kind, d],
            device_id={"head": head_at(d)}, device_id_type=MESH,
        )

    def local_e(kind):
        ref, width = outs[kind]
        return pltpu.make_async_copy(src_e(kind, h), ref.at[:, lanes(h, width)], e_loc.at[kind])

    for d in range(1, heads):
        copy_e(0, d).start()
    local_e(0).start()

    def collect(s, carry):
        copy_d(s).wait_recv()
        own[...] += drecv[s - 1].astype(jnp.float32)
        return carry

    lax.fori_loop(1, jnp.minimum(ctx - 1 - pos, back) + 1, collect, 0)
    dkv[...] = own[...].astype(jnp.bfloat16)
    for kind in (1, 2):
        for d in range(1, heads):
            copy_e(kind, d).start()
        local_e(kind).start()

    for kind in range(4):
        for d in range(1, heads):
            copy_a(kind, d).wait_send()

    def sent_b(s, carry):
        for d in range(heads):
            copy_b(s, d).wait_send()
        return carry

    lax.fori_loop(1, jnp.minimum(ctx - 1 - pos, back) + 1, sent_b, 0)

    def sent_d(s, carry):
        copy_d(s).wait_send()
        return carry

    lax.fori_loop(1, reach + 1, sent_d, 0)
    for kind in range(3):
        local_e(kind).wait()
        for d in range(1, heads):
            copy_e(kind, d).wait_send()
            arrival_e(kind, d).wait_recv()


def solution(mesh):
    heads, outer_n, inner_n = (mesh.shape[a] for a in ("head", "outer", "inner"))

    def body(query_in, key_in, value_in, grad_out):
        rows = query_in.shape[1]
        tok = rows * heads
        back = min((WINDOW + tok - 2) // tok, outer_n * inner_n - 1)
        wide = GROUP * tok
        bf16, f32 = jnp.bfloat16, jnp.float32
        sem = pltpu.SemaphoreType.DMA
        shapes = [(query_in.shape[1:]), (key_in.shape[1:]), (value_in.shape[1:])]
        res = pl.pallas_call(
            functools.partial(kernel, heads, outer_n, inner_n, back),
            out_shape=[jax.ShapeDtypeStruct(s, bf16) for s in shapes],
            in_specs=[pl.BlockSpec(memory_space=pltpu.VMEM)] * 4,
            out_specs=[pl.BlockSpec(memory_space=pltpu.VMEM)] * 3,
            scratch_shapes=[
                pltpu.VMEM((tok, GROUP * HD), bf16),
                pltpu.VMEM((tok, GROUP * HD), bf16),
                pltpu.VMEM((wide, HD), bf16),
                pltpu.VMEM((wide, HD), bf16),
                pltpu.VMEM((back + 1, 2, tok, HD), bf16),
                pltpu.VMEM((back + 1, tok, wide), f32),
                pltpu.VMEM((back + 1, tok, wide), f32),
                pltpu.VMEM((back + 1, tok, wide), bf16),
                pltpu.VMEM((8, wide), f32),
                pltpu.VMEM((8, wide), f32),
                pltpu.VMEM((tok, wide), bf16),
                pltpu.VMEM((tok, wide), bf16),
                pltpu.VMEM((HD, wide), f32),
                pltpu.VMEM((tok, GROUP * HD), bf16),
                pltpu.VMEM((2, tok, HD), bf16),
                pltpu.VMEM((back, 2, tok, HD), bf16),
                pltpu.VMEM((back, 2, tok, HD), bf16),
                pltpu.VMEM((2, tok, HD), f32),
                sem((4, heads)), sem((4, heads)), sem((4,)),
                sem((back + 1, heads)), sem((back + 1, heads)),
                sem((back,)), sem((back,)),
                sem((3, heads)), sem((3, heads)), sem((3,)),
            ],
            compiler_params=pltpu.CompilerParams(
                collective_id=0, has_side_effects=True, vmem_limit_bytes=60 * 1024 * 1024
            ),
        )(query_in[0], key_in[0], value_in[0], grad_out[0])
        return tuple(r[None] for r in res)

    spec = P(("outer", "inner"), "head", None)
    return jax.shard_map(
        body, mesh=mesh, in_specs=(spec,) * 4, out_specs=(spec,) * 3, check_vma=False
    )
```

time: 278 us -> 48.5 us (0.17)
  the two profiles are of different devices: /device:TPU:0 before, /device:TPU:3 now
where the time goes in v1:
time: 48.5 us; the launch traced here: 48.4 us
  Pallas kernels  44.5 us (92%)
  local copies, waits for them, and re-layouts  3.22 us (7%)
  between operations  0.65 us (1%)
    pallas_call x1, Pallas kernels, body(): pl.pallas_call(functools.partial(kernel, heads, outer_n, inner_n, back),...  44.5 us
    unnamed x7, local copies, waits for them, and re-layouts  3.22 us

profile of v1, /device:TPU:3, one launch (start us, length us, event | category | flops | bytes accessed | tf_op | source)
XLA Modules:
  0.0 48.4 jit_solution(15580798248715832833)
XLA Ops:
  0.6 44.5 %shard_map.67 = (bf16[96,1024]{1,0:T(8,128)(2,1)}, bf16[96,512]{1,0:T(8,128)(2,1)}, bf16[96,512]{1,0:T(8,128)(2,1)}) custom-call(bf16[96,1024]{1,0:T(8,128)(2,1)} %bitcast.8, bf16[96,512]{1,0:T(8,128)(2,1)} %bitcast.10, bf16[96,512]{1,0:T(8,128)(2,1)} %bitcast.11, bf16[96,1024]{1,0:T(8,128)(2,1)} %bitcast.9), custom_call_target="tpu_custom_call" | custom-call | tf_op jit(solution)/shard_map/pallas_call | solution.py:287
  45.1 0.0 copy-start.1
  45.1 1.6 %copy.10 = bf16[1,96,1024]{2,1,0:T(8,128)(2,1)} copy(bf16[1,96,1024]{2,1,0:T(8,128)(2,1)} %bitcast.7) | data formatting | bytes 393216
  46.8 0.0 copy-done.1
  46.8 0.0 copy-start
  46.8 0.6 %copy.11 = bf16[1,96,512]{2,1,0:T(8,128)(2,1)} copy(bf16[1,96,512]{2,1,0:T(8,128)(2,1)S(1)} %bitcast.13) | data formatting | bytes 196608
  47.4 0.3 copy-done
  47.7 0.6 %copy.12 = bf16[1,96,512]{2,1,0:T(8,128)(2,1)} copy(bf16[1,96,512]{2,1,0:T(8,128)(2,1)S(1)} %bitcast.12) | data formatting | bytes 196608
Async XLA Ops:
  45.1 1.7 %copy-start.1 = (bf16[96,512]{1,0:T(8,128)(2,1)S(1)}, bf16[96,512]{1,0:T(8,128)(2,1)}, u32[]{:S(2)}) copy-start(bf16[96,512]{1,0:T(8,128)(2,1)} %get-tuple-element.7) | copy-start | bytes 294916
  46.8 0.9 %copy-start = (bf16[96,512]{1,0:T(8,128)(2,1)S(1)}, bf16[96,512]{1,0:T(8,128)(2,1)}, u32[]{:S(2)}) copy-start(bf16[96,512]{1,0:T(8,128)(2,1)} %get-tuple-element.8) | copy-start | bytes 294916

commit v2 on v1

--- a/solution.py
+++ b/solution.py
@@ -115,13 +115,6 @@
             def _():
                 copy_b(s, d).start()
 
-    for kind in (2, 3):
-        local_a(kind).wait()
-        for d in range(1, heads):
-            arrival_a(kind, d).wait_recv()
-    for j in range(GROUP):
-        qst[j * tok:(j + 1) * tok] = qs[:, j * HD:(j + 1) * HD]
-        gst[j * tok:(j + 1) * tok] = gs[:, j * HD:(j + 1) * HD]
     tot[...] = jnp.zeros_like(tot)
     wgt[...] = jnp.zeros_like(wgt)
     dqt[...] = jnp.zeros_like(dqt)
@@ -132,7 +125,6 @@
         for t in range(tok // KT):
             at_t = slice(t * KT, (t + 1) * KT)
             keys = kv[s, 0, at_t]
-            vals = kv[s, 1, at_t]
             for j in range(GROUP):
                 col = slice(j * tok, (j + 1) * tok)
                 capped = jnp.tanh(dot(keys, qst[col], 1, 1) * (QUERY_SCALE / SOFT_CAP))
@@ -144,13 +136,30 @@
                         - lax.broadcasted_iota(jnp.int32, e.shape, 0)
                     )
                     e = jnp.where((apart >= 0) & (apart < WINDOW), e, 0.0)
-                dp = dot(vals, gst[col], 1, 1).astype(jnp.bfloat16)
                 c_all[s, at_t, col] = capped
                 e_all[s, at_t, col] = e
+                tot[:, col] += jnp.sum(e.reshape(KT // 8, 8, tok), axis=0)
+
+    def first_dp(s, carry):
+        for t in range(tok // KT):
+            at_t = slice(t * KT, (t + 1) * KT)
+            vals = kv[s, 1, at_t]
+            for j in range(GROUP):
+                col = slice(j * tok, (j + 1) * tok)
+                dp = dot(vals, gst[col], 1, 1).astype(jnp.bfloat16)
                 d_all[s, at_t, col] = dp
-                tot[:, col] += jnp.sum(e.reshape(KT // 8, 8, tok), axis=0)
-                wgt[:, col] += jnp.sum((e * dp.astype(jnp.float32)).reshape(KT // 8, 8, tok), axis=0)
-
+                weighted = e_all[s, at_t, col] * dp.astype(jnp.float32)
+                wgt[:, col] += jnp.sum(weighted.reshape(KT // 8, 8, tok), axis=0)
+        return carry
+
+    def take(kind, whole, stacked):
+        local_a(kind).wait()
+        for d in range(1, heads):
+            arrival_a(kind, d).wait_recv()
+        for j in range(GROUP):
+            stacked[j * tok:(j + 1) * tok] = whole[:, j * HD:(j + 1) * HD]
+
+    take(2, qs, qst)
     first(0, True)
     reach = jnp.minimum(pos, back)
 
@@ -164,6 +173,8 @@
     lax.fori_loop(1, edge + 1, functools.partial(first_step, False), 0)
     if back > free:
         lax.fori_loop(edge + 1, reach + 1, functools.partial(first_step, True), 0)
+    take(3, gs, gst)
+    lax.fori_loop(0, reach + 1, first_dp, 0)
 
     total = jnp.sum(tot[...], axis=0, keepdims=True)
     inv = 1.0 / total
@@ -172,20 +183,24 @@
     wgt[0:1] = delta
 
     def second(s):
+        dks, dvs = [], []
         for t in range(tok // KT):
             at_t = slice(t * KT, (t + 1) * KT)
+            probs, scs = [], []
             for j in range(GROUP):
                 col = slice(j * tok, (j + 1) * tok)
                 capped = c_all[s, at_t, col]
                 prob = e_all[s, at_t, col] * tot[0:1, col]
-                pb[at_t, col] = prob.astype(jnp.bfloat16)
                 diff = d_all[s, at_t, col].astype(jnp.float32) - wgt[0:1, col]
-                sc[at_t, col] = (
-                    prob * diff * (QUERY_SCALE - QUERY_SCALE * (capped * capped))
-                ).astype(jnp.bfloat16)
-        scaled = sc[...]
-        dqt[...] += dot(kv[s, 0], scaled, 0, 0)
-        return dot(scaled, qst[...], 1, 0), dot(pb[...], gst[...], 1, 0)
+                probs.append(prob.astype(jnp.bfloat16))
+                scs.append(
+                    (prob * diff * (QUERY_SCALE - QUERY_SCALE * (capped * capped))).astype(jnp.bfloat16)
+                )
+            scaled = jnp.concatenate(scs, axis=1)
+            dvs.append(dot(jnp.concatenate(probs, axis=1), gst[...], 1, 0))
+            dks.append(dot(scaled, qst[...], 1, 0))
+            dqt[...] += dot(kv[s, 0, at_t], scaled, 0, 0)
+        return jnp.concatenate(dks, axis=0), jnp.concatenate(dvs, axis=0)
 
     def copy_d(s):
         return pltpu.make_async_remote_copy(
@@ -271,6 +286,19 @@
         for d in range(1, heads):
             copy_e(kind, d).wait_send()
             arrival_e(kind, d).wait_recv()
+
+
+def hand_on(a, b, c, a_to, b_to, c_to, a_via, b_via, c_via, sems):
+    ways = ((a, a_via, a_to), (b, b_via, b_to), (c, c_via, c_to))
+    into = [pltpu.make_async_copy(x, v, sems.at[0, i]) for i, (x, v, _) in enumerate(ways)]
+    out = [pltpu.make_async_copy(v, y, sems.at[1, i]) for i, (_, v, y) in enumerate(ways)]
+    for copy in into:
+        copy.start()
+    for before, after in zip(into, out):
+        before.wait()
+        after.start()
+    for copy in out:
+        copy.wait()
 
 
 def solution(mesh):
@@ -287,8 +315,8 @@
         res = pl.pallas_call(
             functools.partial(kernel, heads, outer_n, inner_n, back),
             out_shape=[jax.ShapeDtypeStruct(s, bf16) for s in shapes],
-            in_specs=[pl.BlockSpec(memory_space=pltpu.VMEM)] * 4,
-            out_specs=[pl.BlockSpec(memory_space=pltpu.VMEM)] * 3,
+            in_specs=[pl.BlockSpec(memory_space=pl.ANY)] * 4,
+            out_specs=[pl.BlockSpec(memory_space=pl.ANY)] * 3,
             scratch_shapes=[
                 pltpu.VMEM((tok, GROUP * HD), bf16),
                 pltpu.VMEM((tok, GROUP * HD), bf16),
@@ -317,6 +345,13 @@
                 collective_id=0, has_side_effects=True, vmem_limit_bytes=60 * 1024 * 1024
             ),
         )(query_in[0], key_in[0], value_in[0], grad_out[0])
+        res = pl.pallas_call(
+            hand_on,
+            out_shape=[jax.ShapeDtypeStruct(s, bf16) for s in shapes],
+            in_specs=[pl.BlockSpec(memory_space=pl.ANY)] * 3,
+            out_specs=[pl.BlockSpec(memory_space=pl.ANY)] * 3,
+            scratch_shapes=[pltpu.VMEM(s, bf16) for s in shapes] + [sem((2, 3))],
+        )(*res)
         return tuple(r[None] for r in res)
 
     spec = P(("outer", "inner"), "head", None)

time: 48.5 us -> 45.6 us (0.940)
  local copies, waits for them, and re-layouts: 3.22 us -> 0 us
    unnamed x7 -> x0, local copies, waits for them, and re-layouts: 3.22 us -> none
    pallas_call x0 -> x1, Pallas kernels: none -> 1.73 us  [body(): pl.pallas_call(hand_on, out_shape=[jax.ShapeDtypeStruct(s, bf16) for s in...]
    pallas_call x1, Pallas kernels: 44.5 us -> 42.8 us  [body(): pl.pallas_call(functools.partial(kernel, heads, outer_n, inner_n, back),...]
where the time goes in v2:
time: 45.6 us; the launch traced here: 45.2 us
  Pallas kernels  44.6 us (98%)
  between operations  0.64 us (1%)
    pallas_call x1, Pallas kernels, body(): pl.pallas_call(functools.partial(kernel, heads, outer_n, inner_n, back),...  42.8 us
    pallas_call x1, Pallas kernels, body(): pl.pallas_call(hand_on, out_shape=[jax.ShapeDtypeStruct(s, bf16) for s in...  1.73 us

profile of v2, /device:TPU:3, one launch (start us, length us, event | category | flops | bytes accessed | tf_op | source)
XLA Modules:
  0.0 45.2 jit_solution(15121762884966116086)
XLA Ops:
  0.6 42.8 %shard_map.67 = (bf16[96,1024]{1,0:T(8,128)(2,1)}, bf16[96,512]{1,0:T(8,128)(2,1)}, bf16[96,512]{1,0:T(8,128)(2,1)}) custom-call(bf16[96,1024]{1,0:T(8,128)(2,1)} %bitcast.7, bf16[96,512]{1,0:T(8,128)(2,1)} %bitcast.9, bf16[96,512]{1,0:T(8,128)(2,1)} %bitcast.10, bf16[96,1024]{1,0:T(8,128)(2,1)} %bitcast.8), custom_call_target="tpu_custom_call" | custom-call | tf_op jit(solution)/shard_map/pallas_call | solution.py:315
  43.5 1.7 %shard_map.68 = (bf16[96,1024]{1,0:T(8,128)(2,1)}, bf16[96,512]{1,0:T(8,128)(2,1)}, bf16[96,512]{1,0:T(8,128)(2,1)}) custom-call(bf16[96,1024]{1,0:T(8,128)(2,1)} %get-tuple-element.9.a, bf16[96,512]{1,0:T(8,128)(2,1)} %get-tuple-element.10.b, bf16[96,512]{1,0:T(8,128)(2,1)} %get-tuple-element.11.c), custom_call_target="tpu_custom_call" | custom-call | tf_op jit(solution)/shard_map/pallas_call | solution.py:348

commit v3 on v2

--- a/solution.py
+++ b/solution.py
@@ -140,16 +140,34 @@
                 e_all[s, at_t, col] = e
                 tot[:, col] += jnp.sum(e.reshape(KT // 8, 8, tok), axis=0)
 
-    def first_dp(s, carry):
+    def copy_d(s, which):
+        return pltpu.make_async_remote_copy(
+            src_ref=dsend.at[s - 1, which], dst_ref=drecv.at[s - 1, which],
+            send_sem=d_ssem.at[s - 1, which], recv_sem=d_rsem.at[s - 1, which],
+            device_id=at(lax.rem(pos - s + ctx, ctx)), device_id_type=MESH,
+        )
+
+    def first_dp(s):
+        dvs = []
         for t in range(tok // KT):
             at_t = slice(t * KT, (t + 1) * KT)
             vals = kv[s, 1, at_t]
+            probs = []
             for j in range(GROUP):
                 col = slice(j * tok, (j + 1) * tok)
                 dp = dot(vals, gst[col], 1, 1).astype(jnp.bfloat16)
                 d_all[s, at_t, col] = dp
-                weighted = e_all[s, at_t, col] * dp.astype(jnp.float32)
+                e = e_all[s, at_t, col]
+                weighted = e * dp.astype(jnp.float32)
                 wgt[:, col] += jnp.sum(weighted.reshape(KT // 8, 8, tok), axis=0)
+                probs.append((e * tot[0:1, col]).astype(jnp.bfloat16))
+            dvs.append(dot(jnp.concatenate(probs, axis=1), gst[...], 1, 0))
+        return jnp.concatenate(dvs, axis=0)
+
+    def first_dp_step(i, carry):
+        s = reach - i
+        dsend[s - 1, 1] = first_dp(s).astype(jnp.bfloat16)
+        copy_d(s, 1).start()
         return carry
 
     def take(kind, whole, stacked):
@@ -173,54 +191,41 @@
     lax.fori_loop(1, edge + 1, functools.partial(first_step, False), 0)
     if back > free:
         lax.fori_loop(edge + 1, reach + 1, functools.partial(first_step, True), 0)
+    inv = 1.0 / jnp.sum(tot[...], axis=0, keepdims=True)
+    tot[0:1] = inv
     take(3, gs, gst)
-    lax.fori_loop(0, reach + 1, first_dp, 0)
-
-    total = jnp.sum(tot[...], axis=0, keepdims=True)
-    inv = 1.0 / total
-    delta = jnp.sum(wgt[...], axis=0, keepdims=True) * inv
-    tot[0:1] = inv
+    lax.fori_loop(0, reach, first_dp_step, 0)
+    own[1] = first_dp(0)
+
+    delta = jnp.sum(wgt[...], axis=0, keepdims=True) * tot[0:1]
     wgt[0:1] = delta
 
     def second(s):
-        dks, dvs = [], []
+        dks = []
         for t in range(tok // KT):
             at_t = slice(t * KT, (t + 1) * KT)
-            probs, scs = [], []
+            scs = []
             for j in range(GROUP):
                 col = slice(j * tok, (j + 1) * tok)
                 capped = c_all[s, at_t, col]
                 prob = e_all[s, at_t, col] * tot[0:1, col]
                 diff = d_all[s, at_t, col].astype(jnp.float32) - wgt[0:1, col]
-                probs.append(prob.astype(jnp.bfloat16))
                 scs.append(
                     (prob * diff * (QUERY_SCALE - QUERY_SCALE * (capped * capped))).astype(jnp.bfloat16)
                 )
             scaled = jnp.concatenate(scs, axis=1)
-            dvs.append(dot(jnp.concatenate(probs, axis=1), gst[...], 1, 0))
             dks.append(dot(scaled, qst[...], 1, 0))
             dqt[...] += dot(kv[s, 0, at_t], scaled, 0, 0)
-        return jnp.concatenate(dks, axis=0), jnp.concatenate(dvs, axis=0)
-
-    def copy_d(s):
-        return pltpu.make_async_remote_copy(
-            src_ref=dsend.at[s - 1], dst_ref=drecv.at[s - 1],
-            send_sem=d_ssem.at[s - 1], recv_sem=d_rsem.at[s - 1],
-            device_id=at(lax.rem(pos - s + ctx, ctx)), device_id_type=MESH,
-        )
+        return jnp.concatenate(dks, axis=0)
 
     def second_step(i, carry):
         s = reach - i
-        dk, dv = second(s)
-        dsend[s - 1, 0] = dk.astype(jnp.bfloat16)
-        dsend[s - 1, 1] = dv.astype(jnp.bfloat16)
-        copy_d(s).start()
+        dsend[s - 1, 0] = second(s).astype(jnp.bfloat16)
+        copy_d(s, 0).start()
         return carry
 
     lax.fori_loop(0, reach, second_step, 0)
-    dk, dv = second(0)
-    own[0] = dk
-    own[1] = dv
+    own[0] = second(0)
     for j in range(GROUP):
         dq[:, j * HD:(j + 1) * HD] = dqt[:, j * tok:(j + 1) * tok].T.astype(jnp.bfloat16)
 
@@ -254,7 +259,8 @@
     local_e(0).start()
 
     def collect(s, carry):
-        copy_d(s).wait_recv()
+        for which in (0, 1):
+            copy_d(s, which).wait_recv()
         own[...] += drecv[s - 1].astype(jnp.float32)
         return carry
 
@@ -277,7 +283,8 @@
     lax.fori_loop(1, jnp.minimum(ctx - 1 - pos, back) + 1, sent_b, 0)
 
     def sent_d(s, carry):
-        copy_d(s).wait_send()
+        for which in (0, 1):
+            copy_d(s, which).wait_send()
         return carry
 
     lax.fori_loop(1, reach + 1, sent_d, 0)
@@ -338,7 +345,7 @@
                 pltpu.VMEM((2, tok, HD), f32),
                 sem((4, heads)), sem((4, heads)), sem((4,)),
                 sem((back + 1, heads)), sem((back + 1, heads)),
-                sem((back,)), sem((back,)),
+                sem((back, 2)), sem((back, 2)),
                 sem((3, heads)), sem((3, heads)), sem((3,)),
             ],
             compiler_params=pltpu.CompilerParams(

time: 45.6 us -> 45 us (0.987)
  no operation moved by 1% of the time
where the time goes in v3:
time: 45 us; the launch traced here: 44.8 us
  Pallas kernels  44.2 us (98%)
  between operations  0.64 us (1%)
    pallas_call x1, Pallas kernels, body(): pl.pallas_call(functools.partial(kernel, heads, outer_n, inner_n, back),...  42.5 us
    pallas_call x1, Pallas kernels, body(): pl.pallas_call(hand_on, out_shape=[jax.ShapeDtypeStruct(s, bf16) for s in...  1.73 us

profile of v3, /device:TPU:3, one launch (start us, length us, event | category | flops | bytes accessed | tf_op | source)
XLA Modules:
  0.0 44.8 jit_solution(11181833972029545896)
XLA Ops:
  0.6 42.5 %shard_map.67 = (bf16[96,1024]{1,0:T(8,128)(2,1)}, bf16[96,512]{1,0:T(8,128)(2,1)}, bf16[96,512]{1,0:T(8,128)(2,1)}) custom-call(bf16[96,1024]{1,0:T(8,128)(2,1)} %bitcast.7, bf16[96,512]{1,0:T(8,128)(2,1)} %bitcast.9, bf16[96,512]{1,0:T(8,128)(2,1)} %bitcast.10, bf16[96,1024]{1,0:T(8,128)(2,1)} %bitcast.8), custom_call_target="tpu_custom_call" | custom-call | tf_op jit(solution)/shard_map/pallas_call | solution.py:322
  43.1 1.7 %shard_map.68 = (bf16[96,1024]{1,0:T(8,128)(2,1)}, bf16[96,512]{1,0:T(8,128)(2,1)}, bf16[96,512]{1,0:T(8,128)(2,1)}) custom-call(bf16[96,1024]{1,0:T(8,128)(2,1)} %get-tuple-element.9.a, bf16[96,512]{1,0:T(8,128)(2,1)} %get-tuple-element.10.b, bf16[96,512]{1,0:T(8,128)(2,1)} %get-tuple-element.11.c), custom_call_target="tpu_custom_call" | custom-call | tf_op jit(solution)/shard_map/pallas_call | solution.py:355

commit v4 on v3

--- a/solution.py
+++ b/solution.py
@@ -258,18 +258,18 @@
         copy_e(0, d).start()
     local_e(0).start()
 
-    def collect(s, carry):
-        for which in (0, 1):
-            copy_d(s, which).wait_recv()
-        own[...] += drecv[s - 1].astype(jnp.float32)
-        return carry
-
-    lax.fori_loop(1, jnp.minimum(ctx - 1 - pos, back) + 1, collect, 0)
-    dkv[...] = own[...].astype(jnp.bfloat16)
-    for kind in (1, 2):
-        for d in range(1, heads):
-            copy_e(kind, d).start()
-        local_e(kind).start()
+    def collect(which, s, carry):
+        copy_d(s, which).wait_recv()
+        own[which] += drecv[s - 1, which].astype(jnp.float32)
+        return carry
+
+    for which in (1, 0):
+        later = jnp.minimum(ctx - 1 - pos, back)
+        lax.fori_loop(1, later + 1, functools.partial(collect, which), 0)
+        dkv[which] = own[which].astype(jnp.bfloat16)
+        for d in range(1, heads):
+            copy_e(which + 1, d).start()
+        local_e(which + 1).start()
 
     for kind in range(4):
         for d in range(1, heads):

time: 45 us -> 42.8 us (0.951)
  Pallas kernels: 44.2 us -> 41.9 us
    pallas_call x1, Pallas kernels: 42.5 us -> 40.2 us  [body(): pl.pallas_call(functools.partial(kernel, heads, outer_n, inner_n, back),...]
where the time goes in v4:
time: 42.8 us; the launch traced here: 42.6 us
  Pallas kernels  41.9 us (98%)
  between operations  0.64 us (1%)
    pallas_call x1, Pallas kernels, body(): pl.pallas_call(functools.partial(kernel, heads, outer_n, inner_n, back),...  40.2 us
    pallas_call x1, Pallas kernels, body(): pl.pallas_call(hand_on, out_shape=[jax.ShapeDtypeStruct(s, bf16) for s in...  1.73 us

profile of v4, /device:TPU:3, one launch (start us, length us, event | category | flops | bytes accessed | tf_op | source)
XLA Modules:
  0.0 42.6 jit_solution(15993483429961513992)
XLA Ops:
  0.6 40.2 %shard_map.67 = (bf16[96,1024]{1,0:T(8,128)(2,1)}, bf16[96,512]{1,0:T(8,128)(2,1)}, bf16[96,512]{1,0:T(8,128)(2,1)}) custom-call(bf16[96,1024]{1,0:T(8,128)(2,1)} %bitcast.7, bf16[96,512]{1,0:T(8,128)(2,1)} %bitcast.9, bf16[96,512]{1,0:T(8,128)(2,1)} %bitcast.10, bf16[96,1024]{1,0:T(8,128)(2,1)} %bitcast.8), custom_call_target="tpu_custom_call" | custom-call | tf_op jit(solution)/shard_map/pallas_call | solution.py:322
  40.8 1.7 %shard_map.68 = (bf16[96,1024]{1,0:T(8,128)(2,1)}, bf16[96,512]{1,0:T(8,128)(2,1)}, bf16[96,512]{1,0:T(8,128)(2,1)}) custom-call(bf16[96,1024]{1,0:T(8,128)(2,1)} %get-tuple-element.9.a, bf16[96,512]{1,0:T(8,128)(2,1)} %get-tuple-element.10.b, bf16[96,512]{1,0:T(8,128)(2,1)} %get-tuple-element.11.c), custom_call_target="tpu_custom_call" | custom-call | tf_op jit(solution)/shard_map/pallas_call | solution.py:355
